TPU v7x, 128 devices: a whole 4x4x4 slice. The times are simulated.
128 devices in a mesh: row: 8 (over z, y_lo), col: 16 (over x, y_hi, core).
Axes of the slice: x: 4, y: 4 (y_hi: 2, y_lo: 2; y = y_hi * 2 + y_lo), z: 4, core: 2. Of those that a mesh axis runs over, the one named last changes fastest.
Arguments:
- t2_amps: bfloat16 [16384, 2048], P('row', 'col'), may hold values from -6 to 6
- v_ints: bfloat16 [2048, 32768], P('row', 'col'), may hold values from -0.125 to 0.125
- t2_mask: int32 [128, 16], P('row', 'col'), may hold values 0 or 1
- v_mask: int32 [16, 256], P('row', 'col'), may hold values 0 or 1
Outputs:
- ladder: bfloat16 [16384, 32768], P('row', 'col')
All inputs are finite; a program needn't handle non-finite values. No bound on the sum of `t2_mask` or of `v_mask` on one device may be relied on, other than what follows from the above.
Results may differ from a plain program's by a relative error of at most 0.001.
Values may be sent and summed in bfloat16 or wider, within the bound.
A program may use at most 64 MiB of HBM per device.

v0:
```python
import jax
import jax.numpy as jnp
from jax import lax
from jax.sharding import PartitionSpec as P

TILE = 128


def expand(mask, rows, cols):
    kept = jnp.broadcast_to(mask[:, None, :, None] > 0, (mask.shape[0], TILE, mask.shape[1], TILE))
    return kept.reshape(rows, cols)


def body(t2_amps, v_ints, t2_mask, v_mask):
    masked_t2 = jnp.where(
        expand(t2_mask, t2_amps.shape[0], t2_amps.shape[1]), t2_amps, jnp.zeros_like(t2_amps)
    )
    masked_v = jnp.where(
        expand(v_mask, v_ints.shape[0], v_ints.shape[1]), v_ints, jnp.zeros_like(v_ints)
    )
    amp_whole = lax.all_gather(masked_t2, "col", axis=1, tiled=True)
    result = jnp.dot(
        amp_whole,
        lax.all_gather(masked_v, "row", axis=0, tiled=True),
        preferred_element_type=jnp.float32,
    )
    return result.astype(jnp.bfloat16)


def solution(mesh):
    in_specs = (P("row", "col"), P("row", "col"), P("row", "col"), P("row", "col"))
    out_specs = P("row", "col")
    return jax.shard_map(body, mesh=mesh, in_specs=in_specs, out_specs=out_specs, check_vma=False)
```

profile of v0, /device:TPU:0, one launch (start us, length us, event | category | flops | bytes accessed | tf_op | source)
XLA Modules:
  0.0 294.6 jit_solution(9353750892337013907)
XLA Ops:
  6.5 0.0 all-gather.5.cloned.1.call-start
  6.5 0.7 broadcast_compare_fusion
  7.2 0.2 broadcast_in_dim.26
  7.4 2.5 bitcast_select_fusion
  9.9 0.0 all-gather.5.cloned.1.call-update
  9.9 0.0 all-gather.3.cloned.1.call-start
  10.0 0.7 compare_bitcast_fusion
  10.6 0.1 broadcast_bitcast_fusion
  10.7 2.2 broadcast_select_fusion
  12.9 0.0 all-gather.3.cloned.1.call-update
  12.9 168.0 %all-gather.5.cloned.1.call-done = bf16[2048,2048]{1,0:T(8,128)(2,1)} async-done(((bf16[256,2048]{1,0:T(8,128)(2,1)}), bf16[2048,2048]{1,0:T(8,128)(2,1)}) %all-gather.5.cloned.1.call-update) | async-done | bytes 8388624 | tf_op jit(solution)/shard_map/all_gather | solution.py:24
  180.9 83.4 %all-gather.3.cloned.1.call-done = bf16[2048,2048]{1,0:T(8,128)(2,1)} async-done(((bf16[2048,128]{1,0:T(8,128)(2,1)}), bf16[2048,2048]{1,0:T(8,128)(2,1)}) %all-gather.3.cloned.1.call-update) | async-done | bytes 8388624 | tf_op jit(solution)/shard_map/all_gather | solution.py:21
  264.3 23.5 %convolution_convert_fusion = bf16[2048,2048]{1,0:T(8,128)(2,1)} fusion(bf16[2048,2048]{1,0:T(8,128)(2,1)} %all-gather.3.cloned.1.call-done, bf16[2048,2048]{1,0:T(8,128)(2,1)} %all-gather.5.cloned.1.call-done), kind=kOutput, calls=%fused_computation | convolution fusion | flops 17184063488 | bytes 25165824 | tf_op jit(solution)/shard_map/dot_general | solution.py:22
Async XLA Ops:
  6.5 174.4 %all-gather.5.cloned.1.call-start = ((), (), s32[]{:S(2)}) async-start(), calls=%async_computation.1 | async-start | bytes 9437184 | tf_op jit(solution)/shard_map/all_gather | solution.py:24
  9.9 254.4 %all-gather.3.cloned.1.call-start = ((), (), s32[]{:S(2)}) async-start(), calls=%async_computation | async-start | bytes 8912896 | tf_op jit(solution)/shard_map/all_gather | solution.py:21
Sparse Core Ops, SparseCore 0:
  10.0 170.8 all-gather.4
  183.2 81.0 all-gather.2
where the time goes:
time: 296 us; the launch traced here: 295 us
  waiting for transfers between devices  251 us (85%)
  matrix products  23.5 us (8%)
  between operations  13.4 us (5%)
  other arithmetic  5.99 us (2%)
    all_gather x1, waiting for transfers between devices, body(): lax.all_gather(masked_v, 'row', axis=0, tiled=True)  168 us
    all_gather x1, waiting for transfers between devices, body(): amp_whole = lax.all_gather(masked_t2, 'col', axis=1, tiled=True)  83.4 us
    dot_general x1, matrix products, body(): jnp.dot(amp_whole, lax.all_gather(masked_v, 'row', axis=0, tiled=True), p...  23.5 us
  transfers between devices with their start and end apart: 2, of which 2 were waited for; matrix products, arithmetic and copies ran while one was open for 1% of the time, Pallas kernels for 0%

commit v1 on v0

v1 whole, which is shorter than its diff:
```python
import jax
import jax.numpy as jnp
from jax import lax
from jax.experimental import pallas as pl
from jax.experimental.pallas import tpu as pltpu
from jax.sharding import PartitionSpec as P

TILE = 128
CHUNK = 256
N_CHUNK = 8
EARLY = 7
PIECE = 256
QROWS = 512
N_Q = 4
CD = 2048
IJ = 2048
MESH = pl.DeviceIdType.MESH


def mask_kernel(t2_mask, v_mask, t2, v, t2_out, v_out):
    for i in range(IJ // TILE):
        rows = pl.ds(i * TILE, TILE)
        block = t2[rows, :]
        t2_out[rows, :] = jnp.where(t2_mask[i, 0] > 0, block, jnp.zeros_like(block))
    for j in range(N_CHUNK):
        for b in range(CHUNK // TILE):
            for i in range(PIECE // TILE):
                rows = pl.ds(i * TILE, TILE)
                block = v[rows, pl.ds(j * CHUNK + b * TILE, TILE)]
                kept = v_mask[i, j * (CHUNK // TILE) + b] > 0
                v_out[j, rows, pl.ds(b * TILE, TILE)] = jnp.where(kept, block, jnp.zeros_like(block))


def product(t_all, v_all, j, rows):
    amps = jnp.concatenate([t_all[p, rows, :] for p in range(CD // TILE)], axis=1)
    return jnp.dot(amps, v_all[j], preferred_element_type=jnp.float32).astype(jnp.bfloat16)


COPIES = {
    "zp_own": N_CHUNK, "zm_own": N_CHUNK, "zp_far": N_CHUNK, "zm_far": N_CHUNK,
    "zp_pair": N_CHUNK, "zm_pair": N_CHUNK, "y_own": N_CHUNK, "y_far": N_CHUNK,
    "t_y": N_Q, "xp_own": N_Q, "xm_own": N_Q, "xp_y": N_Q, "xm_y": N_Q,
    "xp_far": N_Q // 2, "xm_far": N_Q // 2, "xp_yfar": N_Q // 2, "xm_yfar": N_Q // 2,
    "core": 8 * N_Q,
}
FIRST = {}
for _name, _count in COPIES.items():
    FIRST[_name] = sum(COPIES[n] for n in list(COPIES)[: list(COPIES).index(_name)])
N_COPIES = sum(COPIES.values())


def gather_kernel(t_own, v_own, t_all, v_all, early, send, recv, local):
    row, col = lax.axis_index("row"), lax.axis_index("col")
    z, y_lo = row // 2, row % 2
    x, y_hi, core = col // 4, (col // 2) % 2, col % 2

    def at_row(dz, flip=False):
        return ((z + dz) % 4) * 2 + (1 - y_lo if flip else y_lo)

    def at_col(dx, flip=False, other=False):
        return ((x + dx) % 4) * 4 + (1 - y_hi if flip else y_hi) * 2 + (1 - core if other else core)

    to = {
        "zp": (at_row(1), col), "zm": (at_row(3), col), "y": (at_row(0, True), col),
        "xp": (row, at_col(1)), "xm": (row, at_col(3)), "t": (row, at_col(0, True)),
        "core": (row, at_col(0, False, True)),
    }

    def v_slot(j, piece, first=0, count=PIECE):
        return v_all.at[j, pl.ds(pl.multiple_of(piece * PIECE + first, 128), count), :]

    def t_slot(piece, q):
        return t_all.at[piece, pl.ds(q * QROWS, QROWS), :]

    started = []

    def describe(name, n, src, dst):
        i = FIRST[name] + n
        return pltpu.make_async_remote_copy(
            src_ref=src, dst_ref=dst, send_sem=send.at[i], recv_sem=recv.at[i],
            device_id=to[name.split("_")[0]], device_id_type=MESH,
        )

    def put(name, n, src, dst):
        copy = describe(name, n, src, dst)
        copy.start()
        started.append(copy)

    def got(name, n, slot):
        describe(name, n, slot, slot).wait_recv()

    def share(n, q, piece, src=None):
        put("core", n * N_Q + q, t_slot(piece, q) if src is None else src, t_slot(piece, q))

    keep_t = pltpu.make_async_copy(t_own, t_all.at[col], local.at[0])
    keep_v = [pltpu.make_async_copy(v_own.at[j], v_slot(j, row), local.at[1 + j]) for j in range(N_CHUNK)]

    barrier = pltpu.get_barrier_semaphore()
    for device in to.values():
        pl.semaphore_signal(barrier, inc=1, device_id=device, device_id_type=MESH)
    keep_t.start()
    for copy in keep_v:
        copy.start()
    pl.semaphore_wait(barrier, len(to))

    for q in range(N_Q):
        put("t_y", q, t_own.at[pl.ds(q * QROWS, QROWS), :], t_slot(col, q))
    for j in range(N_CHUNK):
        put("zp_own", j, v_own.at[j], v_slot(j, row))
        put("zm_own", j, v_own.at[j], v_slot(j, row))
    for q in range(N_Q):
        put("xp_own", q, t_own.at[pl.ds(q * QROWS, QROWS), :], t_slot(col, q))
        put("xm_own", q, t_own.at[pl.ds(q * QROWS, QROWS), :], t_slot(col, q))
    for j in range(N_CHUNK):
        put("y_own", j, v_own.at[j], v_slot(j, row))
    for q in range(N_Q):
        share(0, q, col, t_own.at[pl.ds(q * QROWS, QROWS), :])

    below, above = at_row(3), at_row(1)
    left, right = at_col(3), at_col(1)
    across = at_col(0, True)
    for j in range(N_CHUNK):
        got("zp_own", j, v_slot(j, below))
        got("zm_own", j, v_slot(j, above))
        put("zp_far", j, v_slot(j, below, 0, 128), v_slot(j, below, 0, 128))
        put("zm_far", j, v_slot(j, above, 128, 128), v_slot(j, above, 128, 128))
        if j < N_Q:
            q = j
            got("xp_own", q, t_slot(left, q))
            got("xm_own", q, t_slot(right, q))
            if q < N_Q // 2:
                put("xp_far", q, t_slot(left, q), t_slot(left, q))
            else:
                put("xm_far", q - N_Q // 2, t_slot(right, q), t_slot(right, q))
            share(1, q, left)
            share(2, q, right)
        else:
            q = j - N_Q
            got("t_y", q, t_slot(across, q))
            put("xp_y", q, t_slot(across, q), t_slot(across, q))
            put("xm_y", q, t_slot(across, q), t_slot(across, q))
            share(3, q, across)

    far = at_col(2)
    for q in range(N_Q):
        if q < N_Q // 2:
            got("xp_far", q, t_slot(far, q))
        else:
            got("xm_far", q - N_Q // 2, t_slot(far, q))
        share(4, q, far)

    pair = at_row(0, True)
    opposite = at_row(2)

    def far_on(j):
        got("zp_far", j, v_slot(j, opposite, 0, 128))
        got("zm_far", j, v_slot(j, opposite, 128, 128))
        put("y_far", j, v_slot(j, opposite), v_slot(j, opposite))

    y_left, y_right, y_far = at_col(3, True), at_col(1, True), at_col(2, True)
    for j in range(N_CHUNK):
        got("y_own", j, v_slot(j, pair))
        put("zp_pair", j, v_slot(j, pair), v_slot(j, pair))
        put("zm_pair", j, v_slot(j, pair), v_slot(j, pair))
        if j < N_Q:
            q = j
            got("xp_y", q, t_slot(y_left, q))
            got("xm_y", q, t_slot(y_right, q))
            if q < N_Q // 2:
                put("xp_yfar", q, t_slot(y_left, q), t_slot(y_left, q))
            else:
                put("xm_yfar", q - N_Q // 2, t_slot(y_right, q), t_slot(y_right, q))
            share(5, q, y_left)
            share(6, q, y_right)
        else:
            far_on(2 * (j - N_Q))
            far_on(2 * (j - N_Q) + 1)
    for q in range(N_Q):
        if q < N_Q // 2:
            got("xp_yfar", q, t_slot(y_far, q))
        else:
            got("xm_yfar", q - N_Q // 2, t_slot(y_far, q))
        share(7, q, y_far)

    other = [at_col(dx, flip, True) for dx, flip in
             ((0, False), (3, False), (1, False), (0, True), (2, False), (3, True), (1, True), (2, True))]
    for n in range(8):
        for q in range(N_Q):
            got("core", n * N_Q + q, t_slot(other[n], q))
    keep_t.wait()
    for copy in keep_v:
        copy.wait()

    def chunk_here(j):
        got("zp_pair", j, v_slot(j, at_row(3, True)))
        got("zm_pair", j, v_slot(j, at_row(1, True)))
        got("y_far", j, v_slot(j, at_row(2, True)))

    for j in range(N_CHUNK):
        chunk_here(j)
        if j < EARLY:
            early[j] = product(t_all, v_all, j, slice(None))
    for copy in started:
        copy.wait_send()


def last_kernel(t_all, v_all, early, out, tail, sems):
    copies = [
        pltpu.make_async_copy(early.at[j], out.at[:, pl.ds(j * CHUNK, CHUNK)], sems.at[j]) for j in range(EARLY)
    ]
    for copy in copies:
        copy.start()
    for j in range(EARLY, N_CHUNK):
        for m in range(2):
            rows = pl.ds(m * (IJ // 2), IJ // 2)
            tail[j - EARLY, rows, :] = product(t_all, v_all, j, rows)
            copy = pltpu.make_async_copy(
                tail.at[j - EARLY, rows, :], out.at[rows, pl.ds(j * CHUNK, CHUNK)],
                sems.at[EARLY + 2 * (j - EARLY) + m],
            )
            copy.start()
            copies.append(copy)
    for copy in copies:
        copy.wait()


def body(t2_amps, v_ints, t2_mask, v_mask):
    bf16 = jnp.bfloat16
    vmem = pl.BlockSpec(memory_space=pltpu.VMEM)
    smem = pl.BlockSpec(memory_space=pltpu.SMEM)
    t_own, v_own = pl.pallas_call(
        mask_kernel,
        out_shape=(pltpu.VMEM((IJ, TILE), bf16), pltpu.VMEM((N_CHUNK, PIECE, CHUNK), bf16)),
        in_specs=[smem, smem, vmem, vmem],
        out_specs=(vmem, vmem),
        compiler_params=pltpu.CompilerParams(vmem_limit_bytes=8 * 2**20),
        name="mask",
    )(t2_mask, v_mask, t2_amps, v_ints)
    inside = lambda a: pltpu.with_memory_space_constraint(a, pltpu.VMEM)
    t_all, v_all, early = pl.pallas_call(
        gather_kernel,
        out_shape=(
            pltpu.VMEM((CD // TILE, IJ, TILE), bf16),
            pltpu.VMEM((N_CHUNK, CD, CHUNK), bf16),
            pltpu.VMEM((EARLY, IJ, CHUNK), bf16),
        ),
        in_specs=[vmem, vmem],
        out_specs=(vmem, vmem, vmem),
        scratch_shapes=[
            pltpu.SemaphoreType.DMA((N_COPIES,)),
            pltpu.SemaphoreType.DMA((N_COPIES,)),
            pltpu.SemaphoreType.DMA((1 + N_CHUNK,)),
        ],
        compiler_params=pltpu.CompilerParams(
            collective_id=0, has_side_effects=True, vmem_limit_bytes=16 * 2**20
        ),
        name="gather",
    )(inside(t_own), inside(v_own))
    return pl.pallas_call(
        last_kernel,
        out_shape=jax.ShapeDtypeStruct((IJ, N_CHUNK * CHUNK), bf16),
        in_specs=[vmem, vmem, vmem],
        out_specs=pl.BlockSpec(memory_space=pl.ANY),
        scratch_shapes=[
            pltpu.VMEM((N_CHUNK - EARLY, IJ, CHUNK), bf16),
            pltpu.SemaphoreType.DMA((EARLY + 2 * (N_CHUNK - EARLY),)),
        ],
        compiler_params=pltpu.CompilerParams(vmem_limit_bytes=16 * 2**20),
        name="last",
    )(inside(t_all), inside(v_all), inside(early))


def solution(mesh):
    in_specs = (P("row", "col"), P("row", "col"), P("row", "col"), P("row", "col"))
    out_specs = P("row", "col")
    return jax.shard_map(body, mesh=mesh, in_specs=in_specs, out_specs=out_specs, check_vma=False)
```

time: 296 us -> 87.7 us (0.30)
  waiting for transfers between devices: 251 us -> 0 us
  Pallas kernels: 0 us -> 83.7 us
  matrix products: 23.5 us -> 0 us
  between operations: 13.4 us -> 0.18 us
  other arithmetic: 5.99 us -> 0 us
  local copies, waits for them, and re-layouts: 0.28 us -> 3.67 us
    all_gather x2 -> x0, waiting for transfers between devices: 251 us -> none  [the longest x1 168 us: body(): lax.all_gather(masked_v, 'row', axis=0, tiled=True)]
    pallas_call x0 -> x3, Pallas kernels: none -> 83.7 us  [the longest x1 78.1 us: body(): pl.pallas_call(gather_kernel, out_shape=(pltpu.VMEM((CD // TILE, IJ, TILE...]
    dot_general x1 -> x0, matrix products: 23.5 us -> none  [body(): jnp.dot(amp_whole, lax.all_gather(masked_v, 'row', axis=0, tiled=True), p...]
    select_n x2 -> x0, other arithmetic: 4.65 us -> none  [the longest x1 2.47 us: body(): jnp.where(expand(v_mask, v_ints.shape[0], v_ints.shape[1]), v_ints, jnp.z...]
    unnamed x0 -> x7, local copies, waits for them, and re-layouts: none -> 3.67 us
  transfers between devices with their start and end apart: 2 -> 0, of which waited for: 2 -> 0; matrix products, arithmetic and copies ran while one was open for 1% -> 0% of each run, Pallas kernels for 0% -> 0%
where the time goes in v1:
time: 87.7 us; the launch traced here: 87.5 us
  Pallas kernels  83.7 us (95%)
  local copies, waits for them, and re-layouts  3.67 us (4%)
    pallas_call x1, Pallas kernels, body(): pl.pallas_call(gather_kernel, out_shape=(pltpu.VMEM((CD // TILE, IJ, TILE...  78.1 us
    pallas_call x1, Pallas kernels, body(): pl.pallas_call(last_kernel, out_shape=jax.ShapeDtypeStruct((IJ, N_CHUNK *...  4.52 us
    unnamed x7, local copies, waits for them, and re-layouts  3.67 us

profile of v1, /device:TPU:0, one launch (start us, length us, event | category | flops | bytes accessed | tf_op | source)
XLA Modules:
  0.0 87.5 jit_solution(4699970429521453726)
XLA Ops:
  0.0 0.7 copy.5.t2_mask
  0.7 0.0 copy-start
  0.7 1.2 %copy-done = bf16[256,2048]{1,0:T(8,128)(2,1)S(1)} copy-done((bf16[256,2048]{1,0:T(8,128)(2,1)S(1)}, bf16[256,2048]{1,0:T(8,128)(2,1)}, u32[]{:S(2)}) %copy-start) | copy-done | bytes 1048600
  2.0 0.0 copy-start.1
  2.0 1.0 %copy-done.1 = bf16[2048,128]{1,0:T(8,128)(2,1)S(1)} copy-done((bf16[2048,128]{1,0:T(8,128)(2,1)S(1)}, bf16[2048,128]{1,0:T(8,128)(2,1)}, u32[]{:S(2)}) %copy-start.1) | copy-done | bytes 524312
  3.0 0.0 copy-start.2
  3.0 0.7 copy-done.2
  3.7 1.1 %mask.1 = (bf16[2048,128]{1,0:T(8,128)(2,1)S(1)}, bf16[8,256,256]{2,1,0:T(8,128)(2,1)S(1)}) custom-call(s32[16,1]{1,0:T(8,128)S(1)} %copy.5.t2_mask, s32[2,16]{1,0:T(2,128)S(1)} %copy-done.2, bf16[2048,128]{1,0:T(8,128)(2,1)S(1)} %copy-done.1, bf16[256,2048]{1,0:T(8,128)(2,1)S(1)} %copy-done), custom_call_target="tpu_custom_call" | custom-call | tf_op jit(solution)/shard_map/mask/pallas_call | solution.py:231
  4.7 78.1 %gather.1 = (bf16[16,2048,128]{2,1,0:T(8,128)(2,1)S(1)}, bf16[8,2048,256]{2,1,0:T(8,128)(2,1)S(1)}, bf16[7,2048,256]{2,1,0:T(8,128)(2,1)S(1)}) custom-call(bf16[2048,128]{1,0:T(8,128)(2,1)S(1)} %get-tuple-element.10.t_own, bf16[8,256,256]{2,1,0:T(8,128)(2,1)S(1)} %get-tuple-element.11.v_own), custom_call_target="tpu_custom_call" | custom-call | tf_op jit(solution)/shard_map/gather/pallas_call | solution.py:240
  82.8 4.5 %last.1 = bf16[2048,2048]{1,0:T(8,128)(2,1)} custom-call(bf16[16,2048,128]{2,1,0:T(8,128)(2,1)S(1)} %get-tuple-element.12.t_all, bf16[8,2048,256]{2,1,0:T(8,128)(2,1)S(1)} %get-tuple-element.13.v_all, bf16[7,2048,256]{2,1,0:T(8,128)(2,1)S(1)} %get-tuple-element.14.early), custom_call_target="tpu_custom_call" | custom-call | tf_op jit(solution)/shard_map/last/pallas_call | solution.py:259
Async XLA Ops:
  0.7 1.2 %copy-start = (bf16[256,2048]{1,0:T(8,128)(2,1)S(1)}, bf16[256,2048]{1,0:T(8,128)(2,1)}, u32[]{:S(2)}) copy-start(bf16[256,2048]{1,0:T(8,128)(2,1)} %v.1) | copy-start | bytes 3145732
  2.0 1.0 %copy-start.1 = (bf16[2048,128]{1,0:T(8,128)(2,1)S(1)}, bf16[2048,128]{1,0:T(8,128)(2,1)}, u32[]{:S(2)}) copy-start(bf16[2048,128]{1,0:T(8,128)(2,1)} %t2.1) | copy-start | bytes 1572868
  3.0 0.7 copy-start.2

commit v2 on v1

--- a/solution.py
+++ b/solution.py
@@ -9,6 +9,7 @@
 CHUNK = 256
 N_CHUNK = 8
 EARLY = 7
+Y_FIRST = 3
 PIECE = 256
 QROWS = 512
 N_Q = 4
@@ -17,15 +18,30 @@
 MESH = pl.DeviceIdType.MESH
 
 
-def mask_kernel(t2_mask, v_mask, t2, v, t2_out, v_out):
+def mask_kernel(t2_mask, v_mask, t2_hbm, v_hbm, t2_out, v_out, t2, v, sems):
+    v_in = [
+        pltpu.make_async_copy(v_hbm.at[pl.ds(i * TILE, TILE), :], v.at[pl.ds(i * TILE, TILE), :], sems.at[i])
+        for i in range(PIECE // TILE)
+    ]
+    t_in = [
+        pltpu.make_async_copy(
+            t2_hbm.at[pl.ds(q * QROWS, QROWS), :], t2.at[pl.ds(q * QROWS, QROWS), :], sems.at[PIECE // TILE + q]
+        )
+        for q in range(N_Q)
+    ]
+    for copy in t_in + v_in:
+        copy.start()
     for i in range(IJ // TILE):
+        if i % (QROWS // TILE) == 0:
+            t_in[i // (QROWS // TILE)].wait()
         rows = pl.ds(i * TILE, TILE)
         block = t2[rows, :]
-        t2_out[rows, :] = jnp.where(t2_mask[i, 0] > 0, block, jnp.zeros_like(block))
-    for j in range(N_CHUNK):
-        for b in range(CHUNK // TILE):
-            for i in range(PIECE // TILE):
-                rows = pl.ds(i * TILE, TILE)
+        t2_out[rows, :] = jnp.where(t2_mask[i] > 0, block, jnp.zeros_like(block))
+    for i in range(PIECE // TILE):
+        v_in[i].wait()
+        rows = pl.ds(i * TILE, TILE)
+        for j in range(N_CHUNK):
+            for b in range(CHUNK // TILE):
                 block = v[rows, pl.ds(j * CHUNK + b * TILE, TILE)]
                 kept = v_mask[i, j * (CHUNK // TILE) + b] > 0
                 v_out[j, rows, pl.ds(b * TILE, TILE)] = jnp.where(kept, block, jnp.zeros_like(block))
@@ -39,7 +55,7 @@
 COPIES = {
     "zp_own": N_CHUNK, "zm_own": N_CHUNK, "zp_far": N_CHUNK, "zm_far": N_CHUNK,
     "zp_pair": N_CHUNK, "zm_pair": N_CHUNK, "y_own": N_CHUNK, "y_far": N_CHUNK,
-    "t_y": N_Q, "xp_own": N_Q, "xm_own": N_Q, "xp_y": N_Q, "xm_y": N_Q,
+    "b_t": N_Q, "y_t": N_Q, "xp_own": N_Q, "xm_own": N_Q, "xp_y": N_Q, "xm_y": N_Q,
     "xp_far": N_Q // 2, "xm_far": N_Q // 2, "xp_yfar": N_Q // 2, "xm_yfar": N_Q // 2,
     "core": 8 * N_Q,
 }
@@ -49,7 +65,7 @@
 N_COPIES = sum(COPIES.values())
 
 
-def gather_kernel(t_own, v_own, t_all, v_all, early, send, recv, local):
+def gather_kernel(t_own, v_own, t_all, v_all, early, relay, send, recv, local):
     row, col = lax.axis_index("row"), lax.axis_index("col")
     z, y_lo = row // 2, row % 2
     x, y_hi, core = col // 4, (col // 2) % 2, col % 2
@@ -62,7 +78,7 @@
 
     to = {
         "zp": (at_row(1), col), "zm": (at_row(3), col), "y": (at_row(0, True), col),
-        "xp": (row, at_col(1)), "xm": (row, at_col(3)), "t": (row, at_col(0, True)),
+        "xp": (row, at_col(1)), "xm": (row, at_col(3)), "b": (at_row(0, True), at_col(0, True)),
         "core": (row, at_col(0, False, True)),
     }
 
@@ -103,43 +119,58 @@
         copy.start()
     pl.semaphore_wait(barrier, len(to))
 
-    for q in range(N_Q):
-        put("t_y", q, t_own.at[pl.ds(q * QROWS, QROWS), :], t_slot(col, q))
+    def own_q(q):
+        return t_own.at[pl.ds(q * QROWS, QROWS), :]
+
+    def relay_q(q):
+        return relay.at[pl.ds(q * QROWS, QROWS), :]
+
+    def y_own(j):
+        put("y_own", j, v_own.at[j], v_slot(j, row))
+
+    for j in range(Y_FIRST):
+        y_own(j)
+    for q in range(N_Q):
+        put("b_t", q, own_q(q), relay_q(q))
     for j in range(N_CHUNK):
         put("zp_own", j, v_own.at[j], v_slot(j, row))
         put("zm_own", j, v_own.at[j], v_slot(j, row))
     for q in range(N_Q):
-        put("xp_own", q, t_own.at[pl.ds(q * QROWS, QROWS), :], t_slot(col, q))
-        put("xm_own", q, t_own.at[pl.ds(q * QROWS, QROWS), :], t_slot(col, q))
-    for j in range(N_CHUNK):
-        put("y_own", j, v_own.at[j], v_slot(j, row))
-    for q in range(N_Q):
-        share(0, q, col, t_own.at[pl.ds(q * QROWS, QROWS), :])
+        put("xp_own", q, own_q(q), t_slot(col, q))
+        put("xm_own", q, own_q(q), t_slot(col, q))
+    for q in range(N_Q):
+        share(0, q, col, own_q(q))
 
     below, above = at_row(3), at_row(1)
     left, right = at_col(3), at_col(1)
     across = at_col(0, True)
-    for j in range(N_CHUNK):
+
+    def v_far(j):
         got("zp_own", j, v_slot(j, below))
         got("zm_own", j, v_slot(j, above))
         put("zp_far", j, v_slot(j, below, 0, 128), v_slot(j, below, 0, 128))
         put("zm_far", j, v_slot(j, above, 128, 128), v_slot(j, above, 128, 128))
-        if j < N_Q:
-            q = j
-            got("xp_own", q, t_slot(left, q))
-            got("xm_own", q, t_slot(right, q))
-            if q < N_Q // 2:
-                put("xp_far", q, t_slot(left, q), t_slot(left, q))
-            else:
-                put("xm_far", q - N_Q // 2, t_slot(right, q), t_slot(right, q))
-            share(1, q, left)
-            share(2, q, right)
+
+    for q in range(N_Q):
+        got("b_t", q, relay_q(q))
+        put("y_t", q, relay_q(q), t_slot(across, q))
+        got("xp_own", q, t_slot(left, q))
+        got("xm_own", q, t_slot(right, q))
+        if q < N_Q // 2:
+            put("xp_far", q, t_slot(left, q), t_slot(left, q))
         else:
-            q = j - N_Q
-            got("t_y", q, t_slot(across, q))
-            put("xp_y", q, t_slot(across, q), t_slot(across, q))
-            put("xm_y", q, t_slot(across, q), t_slot(across, q))
-            share(3, q, across)
+            put("xm_far", q - N_Q // 2, t_slot(right, q), t_slot(right, q))
+        share(1, q, left)
+        share(2, q, right)
+        v_far(q)
+    for j in range(Y_FIRST, N_CHUNK):
+        y_own(j)
+    for q in range(N_Q):
+        got("y_t", q, t_slot(across, q))
+        put("xp_y", q, t_slot(across, q), t_slot(across, q))
+        put("xm_y", q, t_slot(across, q), t_slot(across, q))
+        share(3, q, across)
+        v_far(N_Q + q)
 
     far = at_col(2)
     for q in range(N_Q):
@@ -227,15 +258,21 @@
 def body(t2_amps, v_ints, t2_mask, v_mask):
     bf16 = jnp.bfloat16
     vmem = pl.BlockSpec(memory_space=pltpu.VMEM)
+    hbm = pl.BlockSpec(memory_space=pltpu.HBM)
     smem = pl.BlockSpec(memory_space=pltpu.SMEM)
     t_own, v_own = pl.pallas_call(
         mask_kernel,
         out_shape=(pltpu.VMEM((IJ, TILE), bf16), pltpu.VMEM((N_CHUNK, PIECE, CHUNK), bf16)),
-        in_specs=[smem, smem, vmem, vmem],
+        in_specs=[smem, smem, hbm, hbm],
         out_specs=(vmem, vmem),
-        compiler_params=pltpu.CompilerParams(vmem_limit_bytes=8 * 2**20),
+        scratch_shapes=[
+            pltpu.VMEM((IJ, TILE), bf16),
+            pltpu.VMEM((PIECE, N_CHUNK * CHUNK), bf16),
+            pltpu.SemaphoreType.DMA((PIECE // TILE + N_Q,)),
+        ],
+        compiler_params=pltpu.CompilerParams(vmem_limit_bytes=62 * 2**20),
         name="mask",
-    )(t2_mask, v_mask, t2_amps, v_ints)
+    )(t2_mask.reshape(IJ // TILE), v_mask, t2_amps, v_ints)
     inside = lambda a: pltpu.with_memory_space_constraint(a, pltpu.VMEM)
     t_all, v_all, early = pl.pallas_call(
         gather_kernel,
@@ -247,6 +284,7 @@
         in_specs=[vmem, vmem],
         out_specs=(vmem, vmem, vmem),
         scratch_shapes=[
+            pltpu.VMEM((IJ, TILE), bf16),
             pltpu.SemaphoreType.DMA((N_COPIES,)),
             pltpu.SemaphoreType.DMA((N_COPIES,)),
             pltpu.SemaphoreType.DMA((1 + N_CHUNK,)),

time: 87.7 us -> 85.2 us (0.971)
  local copies, waits for them, and re-layouts: 3.67 us -> 0 us
  Pallas kernels: 83.7 us -> 84.9 us
    unnamed x7 -> x0, local copies, waits for them, and re-layouts: 3.67 us -> none
    pallas_call x1, Pallas kernels: 1.06 us -> 2.34 us  [body(): pl.pallas_call(mask_kernel, out_shape=(pltpu.VMEM((IJ, TILE), bf16), pltp...]
where the time goes in v2:
time: 85.2 us; the launch traced here: 85 us
  Pallas kernels  84.9 us (100%)
    pallas_call x1, Pallas kernels, body(): pl.pallas_call(gather_kernel, out_shape=(pltpu.VMEM((CD // TILE, IJ, TILE...  78 us
    pallas_call x1, Pallas kernels, body(): pl.pallas_call(last_kernel, out_shape=jax.ShapeDtypeStruct((IJ, N_CHUNK *...  4.53 us
    pallas_call x1, Pallas kernels, body(): pl.pallas_call(mask_kernel, out_shape=(pltpu.VMEM((IJ, TILE), bf16), pltp...  2.34 us

profile of v2, /device:TPU:0, one launch (start us, length us, event | category | flops | bytes accessed | tf_op | source)
XLA Modules:
  0.0 85.0 jit_solution(8362663976076788736)
XLA Ops:
  0.0 2.3 %mask.1 = (bf16[2048,128]{1,0:T(8,128)(2,1)S(1)}, bf16[8,256,256]{2,1,0:T(8,128)(2,1)S(1)}) custom-call(s32[16]{0:T(128)} %bitcast.1, s32[2,16]{1,0:T(2,128)} %v_mask.1, bf16[2048,128]{1,0:T(8,128)(2,1)} %t2_hbm.1, bf16[256,2048]{1,0:T(8,128)(2,1)} %v_hbm.1), custom_call_target="tpu_custom_call" | custom-call | tf_op jit(solution)/shard_map/mask/pallas_call | solution.py:263
  2.3 78.0 %gather.1 = (bf16[16,2048,128]{2,1,0:T(8,128)(2,1)S(1)}, bf16[8,2048,256]{2,1,0:T(8,128)(2,1)S(1)}, bf16[7,2048,256]{2,1,0:T(8,128)(2,1)S(1)}) custom-call(bf16[2048,128]{1,0:T(8,128)(2,1)S(1)} %get-tuple-element.10.t_own, bf16[8,256,256]{2,1,0:T(8,128)(2,1)S(1)} %get-tuple-element.11.v_own), custom_call_target="tpu_custom_call" | custom-call | tf_op jit(solution)/shard_map/gather/pallas_call | solution.py:277
  80.4 4.5 %last.1 = bf16[2048,2048]{1,0:T(8,128)(2,1)} custom-call(bf16[16,2048,128]{2,1,0:T(8,128)(2,1)S(1)} %get-tuple-element.12.t_all, bf16[8,2048,256]{2,1,0:T(8,128)(2,1)S(1)} %get-tuple-element.13.v_all, bf16[7,2048,256]{2,1,0:T(8,128)(2,1)S(1)} %get-tuple-element.14.early), custom_call_target="tpu_custom_call" | custom-call | tf_op jit(solution)/shard_map/last/pallas_call | solution.py:297

commit v3 on v2

--- a/solution.py
+++ b/solution.py
@@ -8,7 +8,6 @@
 TILE = 128
 CHUNK = 256
 N_CHUNK = 8
-EARLY = 7
 Y_FIRST = 3
 PIECE = 256
 QROWS = 512
@@ -47,9 +46,12 @@
                 v_out[j, rows, pl.ds(b * TILE, TILE)] = jnp.where(kept, block, jnp.zeros_like(block))
 
 
-def product(t_all, v_all, j, rows):
-    amps = jnp.concatenate([t_all[p, rows, :] for p in range(CD // TILE)], axis=1)
-    return jnp.dot(amps, v_all[j], preferred_element_type=jnp.float32).astype(jnp.bfloat16)
+def product(t_all, v_all, j, rows, pieces):
+    amps = jnp.concatenate([t_all[2 * p + h, rows, :] for p in pieces for h in range(2)], axis=1)
+    ints = jnp.concatenate(
+        [v_all[j, pl.ds(pl.multiple_of(p * PIECE, PIECE), PIECE), :] for p in pieces], axis=0
+    )
+    return jnp.dot(amps, ints, preferred_element_type=jnp.float32)
 
 
 COPIES = {
@@ -65,7 +67,7 @@
 N_COPIES = sum(COPIES.values())
 
 
-def gather_kernel(t_own, v_own, t_all, v_all, early, relay, send, recv, local):
+def gather_kernel(t_own, v_own, early, t_all, v_all, partial, relay, send, recv, local):
     row, col = lax.axis_index("row"), lax.axis_index("col")
     z, y_lo = row // 2, row % 2
     x, y_hi, core = col // 4, (col // 2) % 2, col % 2
@@ -228,29 +230,26 @@
         got("y_far", j, v_slot(j, at_row(2, True)))
 
     for j in range(N_CHUNK):
+        for q in range(N_Q):
+            rows = pl.ds(q * QROWS, QROWS)
+            partial[j, rows, :] = product(t_all, v_all, j, rows, (row, below, above, opposite, pair))
+    late = (at_row(3, True), at_row(1, True), at_row(2, True))
+    for j in range(N_CHUNK):
         chunk_here(j)
-        if j < EARLY:
-            early[j] = product(t_all, v_all, j, slice(None))
+        for q in range(N_Q):
+            rows = pl.ds(q * QROWS, QROWS)
+            whole = partial[j, rows, :] + product(t_all, v_all, j, rows, late)
+            early[j, rows, :] = whole.astype(jnp.bfloat16)
     for copy in started:
         copy.wait_send()
 
 
-def last_kernel(t_all, v_all, early, out, tail, sems):
+def last_kernel(early, out, sems):
     copies = [
-        pltpu.make_async_copy(early.at[j], out.at[:, pl.ds(j * CHUNK, CHUNK)], sems.at[j]) for j in range(EARLY)
+        pltpu.make_async_copy(early.at[j], out.at[:, pl.ds(j * CHUNK, CHUNK)], sems.at[j]) for j in range(N_CHUNK)
     ]
     for copy in copies:
         copy.start()
-    for j in range(EARLY, N_CHUNK):
-        for m in range(2):
-            rows = pl.ds(m * (IJ // 2), IJ // 2)
-            tail[j - EARLY, rows, :] = product(t_all, v_all, j, rows)
-            copy = pltpu.make_async_copy(
-                tail.at[j - EARLY, rows, :], out.at[rows, pl.ds(j * CHUNK, CHUNK)],
-                sems.at[EARLY + 2 * (j - EARLY) + m],
-            )
-            copy.start()
-            copies.append(copy)
     for copy in copies:
         copy.wait()
 
@@ -274,38 +273,34 @@
         name="mask",
     )(t2_mask.reshape(IJ // TILE), v_mask, t2_amps, v_ints)
     inside = lambda a: pltpu.with_memory_space_constraint(a, pltpu.VMEM)
-    t_all, v_all, early = pl.pallas_call(
+    early = pl.pallas_call(
         gather_kernel,
-        out_shape=(
+        out_shape=pltpu.VMEM((N_CHUNK, IJ, CHUNK), bf16),
+        in_specs=[vmem, vmem],
+        out_specs=vmem,
+        scratch_shapes=[
             pltpu.VMEM((CD // TILE, IJ, TILE), bf16),
             pltpu.VMEM((N_CHUNK, CD, CHUNK), bf16),
-            pltpu.VMEM((EARLY, IJ, CHUNK), bf16),
-        ),
-        in_specs=[vmem, vmem],
-        out_specs=(vmem, vmem, vmem),
-        scratch_shapes=[
+            pltpu.VMEM((N_CHUNK, IJ, CHUNK), jnp.float32),
             pltpu.VMEM((IJ, TILE), bf16),
             pltpu.SemaphoreType.DMA((N_COPIES,)),
             pltpu.SemaphoreType.DMA((N_COPIES,)),
             pltpu.SemaphoreType.DMA((1 + N_CHUNK,)),
         ],
         compiler_params=pltpu.CompilerParams(
-            collective_id=0, has_side_effects=True, vmem_limit_bytes=16 * 2**20
+            collective_id=0, has_side_effects=True, vmem_limit_bytes=48 * 2**20
         ),
         name="gather",
     )(inside(t_own), inside(v_own))
     return pl.pallas_call(
         last_kernel,
         out_shape=jax.ShapeDtypeStruct((IJ, N_CHUNK * CHUNK), bf16),
-        in_specs=[vmem, vmem, vmem],
+        in_specs=[vmem],
         out_specs=pl.BlockSpec(memory_space=pl.ANY),
-        scratch_shapes=[
-            pltpu.VMEM((N_CHUNK - EARLY, IJ, CHUNK), bf16),
-            pltpu.SemaphoreType.DMA((EARLY + 2 * (N_CHUNK - EARLY),)),
-        ],
+        scratch_shapes=[pltpu.SemaphoreType.DMA((N_CHUNK,))],
         compiler_params=pltpu.CompilerParams(vmem_limit_bytes=16 * 2**20),
         name="last",
-    )(inside(t_all), inside(v_all), inside(early))
+    )(inside(early))
 
 
 def solution(mesh):

time: 85.2 us -> 73.3 us (0.86)
  Pallas kernels: 84.9 us -> 73.1 us
    pallas_call x1, Pallas kernels: 78 us -> 67.4 us  [body(): pl.pallas_call(gather_kernel, out_shape=pltpu.VMEM((N_CHUNK, IJ, CHUNK),...]
    pallas_call x1, Pallas kernels: 4.53 us -> 3.37 us  [body(): pl.pallas_call(last_kernel, out_shape=jax.ShapeDtypeStruct((IJ, N_CHUNK *...]
where the time goes in v3:
time: 73.3 us; the launch traced here: 73.2 us
  Pallas kernels  73.1 us (100%)
    pallas_call x1, Pallas kernels, body(): pl.pallas_call(gather_kernel, out_shape=pltpu.VMEM((N_CHUNK, IJ, CHUNK),...  67.4 us
    pallas_call x1, Pallas kernels, body(): pl.pallas_call(last_kernel, out_shape=jax.ShapeDtypeStruct((IJ, N_CHUNK *...  3.37 us
    pallas_call x1, Pallas kernels, body(): pl.pallas_call(mask_kernel, out_shape=(pltpu.VMEM((IJ, TILE), bf16), pltp...  2.34 us

profile of v3, /device:TPU:0, one launch (start us, length us, event | category | flops | bytes accessed | tf_op | source)
XLA Modules:
  0.0 73.2 jit_solution(2162010691156391002)
XLA Ops:
  0.0 2.3 %mask.1 = (bf16[2048,128]{1,0:T(8,128)(2,1)S(1)}, bf16[8,256,256]{2,1,0:T(8,128)(2,1)S(1)}) custom-call(s32[16]{0:T(128)} %bitcast.1, s32[2,16]{1,0:T(2,128)} %v_mask.1, bf16[2048,128]{1,0:T(8,128)(2,1)} %t2_hbm.1, bf16[256,2048]{1,0:T(8,128)(2,1)} %v_hbm.1), custom_call_target="tpu_custom_call" | custom-call | tf_op jit(solution)/shard_map/mask/pallas_call | solution.py:262
  2.3 67.4 %gather.1.early = bf16[8,2048,256]{2,1,0:T(8,128)(2,1)S(1)} custom-call(bf16[2048,128]{1,0:T(8,128)(2,1)S(1)} %get-tuple-element.7.t_own, bf16[8,256,256]{2,1,0:T(8,128)(2,1)S(1)} %get-tuple-element.8.v_own), custom_call_target="tpu_custom_call" | custom-call | tf_op jit(solution)/shard_map/gather/pallas_call | solution.py:276
  69.8 3.4 %last.1 = bf16[2048,2048]{1,0:T(8,128)(2,1)} custom-call(bf16[8,2048,256]{2,1,0:T(8,128)(2,1)S(1)} %gather.1.early), custom_call_target="tpu_custom_call" | custom-call | tf_op jit(solution)/shard_map/last/pallas_call | solution.py:295

commit v4 on v3

--- a/solution.py
+++ b/solution.py
@@ -192,9 +192,6 @@
 
     y_left, y_right, y_far = at_col(3, True), at_col(1, True), at_col(2, True)
     for j in range(N_CHUNK):
-        got("y_own", j, v_slot(j, pair))
-        put("zp_pair", j, v_slot(j, pair), v_slot(j, pair))
-        put("zm_pair", j, v_slot(j, pair), v_slot(j, pair))
         if j < N_Q:
             q = j
             got("xp_y", q, t_slot(y_left, q))
@@ -205,9 +202,10 @@
                 put("xm_yfar", q - N_Q // 2, t_slot(y_right, q), t_slot(y_right, q))
             share(5, q, y_left)
             share(6, q, y_right)
-        else:
-            far_on(2 * (j - N_Q))
-            far_on(2 * (j - N_Q) + 1)
+        far_on(j)
+        got("y_own", j, v_slot(j, pair))
+        put("zp_pair", j, v_slot(j, pair), v_slot(j, pair))
+        put("zm_pair", j, v_slot(j, pair), v_slot(j, pair))
     for q in range(N_Q):
         if q < N_Q // 2:
             got("xp_yfar", q, t_slot(y_far, q))
@@ -239,14 +237,15 @@
         for q in range(N_Q):
             rows = pl.ds(q * QROWS, QROWS)
             whole = partial[j, rows, :] + product(t_all, v_all, j, rows, late)
-            early[j, rows, :] = whole.astype(jnp.bfloat16)
+            early[rows, pl.ds(j * CHUNK, CHUNK)] = whole.astype(jnp.bfloat16)
     for copy in started:
         copy.wait_send()
 
 
 def last_kernel(early, out, sems):
     copies = [
-        pltpu.make_async_copy(early.at[j], out.at[:, pl.ds(j * CHUNK, CHUNK)], sems.at[j]) for j in range(N_CHUNK)
+        pltpu.make_async_copy(early.at[pl.ds(j * 256, 256), :], out.at[pl.ds(j * 256, 256), :], sems.at[j])
+        for j in range(N_CHUNK)
     ]
     for copy in copies:
         copy.start()
@@ -275,7 +274,7 @@
     inside = lambda a: pltpu.with_memory_space_constraint(a, pltpu.VMEM)
     early = pl.pallas_call(
         gather_kernel,
-        out_shape=pltpu.VMEM((N_CHUNK, IJ, CHUNK), bf16),
+        out_shape=pltpu.VMEM((IJ, N_CHUNK * CHUNK), bf16),
         in_specs=[vmem, vmem],
         out_specs=vmem,
         scratch_shapes=[

time: 73.3 us -> 73.3 us (level)
  no operation moved by 1% of the time
where the time goes in v4:
time: 73.3 us; the launch traced here: 73.2 us
  Pallas kernels  73.1 us (100%)
    pallas_call x1, Pallas kernels, body(): pl.pallas_call(gather_kernel, out_shape=pltpu.VMEM((IJ, N_CHUNK * CHUNK),...  67.4 us
    pallas_call x1, Pallas kernels, body(): pl.pallas_call(last_kernel, out_shape=jax.ShapeDtypeStruct((IJ, N_CHUNK *...  3.37 us
    pallas_call x1, Pallas kernels, body(): pl.pallas_call(mask_kernel, out_shape=(pltpu.VMEM((IJ, TILE), bf16), pltp...  2.34 us

profile of v4, /device:TPU:0, one launch (start us, length us, event | category | flops | bytes accessed | tf_op | source)
XLA Modules:
  0.0 73.2 jit_solution(5216115165647577460)
XLA Ops:
  0.0 2.3 %mask.1 = (bf16[2048,128]{1,0:T(8,128)(2,1)S(1)}, bf16[8,256,256]{2,1,0:T(8,128)(2,1)S(1)}) custom-call(s32[16]{0:T(128)} %bitcast.1, s32[2,16]{1,0:T(2,128)} %v_mask.1, bf16[2048,128]{1,0:T(8,128)(2,1)} %t2_hbm.1, bf16[256,2048]{1,0:T(8,128)(2,1)} %v_hbm.1), custom_call_target="tpu_custom_call" | custom-call | tf_op jit(solution)/shard_map/mask/pallas_call | solution.py:261
  2.3 67.4 %gather.1.early = bf16[2048,2048]{1,0:T(8,128)(2,1)S(1)} custom-call(bf16[2048,128]{1,0:T(8,128)(2,1)S(1)} %get-tuple-element.7.t_own, bf16[8,256,256]{2,1,0:T(8,128)(2,1)S(1)} %get-tuple-element.8.v_own), custom_call_target="tpu_custom_call" | custom-call | tf_op jit(solution)/shard_map/gather/pallas_call | solution.py:275
  69.8 3.4 %last.1 = bf16[2048,2048]{1,0:T(8,128)(2,1)} custom-call(bf16[2048,2048]{1,0:T(8,128)(2,1)S(1)} %gather.1.early), custom_call_target="tpu_custom_call" | custom-call | tf_op jit(solution)/shard_map/last/pallas_call | solution.py:294
